TPU v7x, 32 devices: a whole 2x2x4 slice. The times are simulated.
32 devices in a mesh: replica: 8 (over y, x, core), tok: 4 (over z).
Axes of the slice: x: 2, y: 2, z: 4, core: 2. Of those that a mesh axis runs over, the one named last changes fastest.
Arguments:
- activations: bfloat16 [8192, 2880], P(('replica', 'tok')), may hold values from -6 to 6
- cotangent: bfloat16 [8192, 512], P(('replica', 'tok')), may hold values from -6 to 6
- next_inputs: bfloat16 [8192, 2880], P(('replica', 'tok')), may hold values from -6 to 6
- weight_tiles: bfloat16 [360, 4096], P('tok'), may hold values from -0.109375 to 0.109375
- momentum: float32 [8, 360, 4096], P('replica', 'tok'), may hold values from -6 to 6
- chosen: int32 [8, 4, 8], P('replica', 'tok'), may hold values from 0 to 89, as said below
- counts: int32 [8, 4], P('replica', 'tok'), may hold values from 1 to 8, as said below
Outputs:
- values: bfloat16 [8192, 512], P(('replica', 'tok'))
- new_momentum: float32 [8, 360, 4096], P('replica', 'tok')
Inputs may be any that keep to these rules, and one draw needn't show every extreme that they name: Each list chosen[r, k] names 8 different tile numbers of the shard's 90 tiles; only the first counts[r, k] of them are selected. `counts`: in every draw some token shard has 8 selected tiles in every replica.
All inputs are finite; a program needn't handle non-finite values.
Results may differ from a plain program's by a relative error of at most 0.015.
Values may be sent and summed in bfloat16 or wider, within the bound.
No kernel may reach another device: no remote copies, remote signals or barrier semaphores. Data moves between devices by JAX's collectives and lax.ppermute only.
A program may use at most 64 MiB of HBM per device.

v0:
```python
import math

import jax
import jax.numpy as jnp
from jax import lax
from jax.sharding import PartitionSpec as P

TILE = 64
KEEP = 32


momentum_decay = 0.9
step_size = 0.01


def cosine_rows(count):
    frequency = jnp.arange(count, dtype=jnp.float32)[:, None]
    position = jnp.arange(TILE, dtype=jnp.float32)[None, :]
    cosines = jnp.cos(math.pi * (2.0 * position + 1.0) * frequency / (2.0 * TILE))
    factor = jnp.where(frequency == 0, math.sqrt(1.0 / TILE), math.sqrt(2.0 / TILE))
    return cosines * factor


def rebuild(summed, weight_part, keep_rows):
    quads = summed.reshape(summed.shape[0], KEEP, KEEP)
    update = jnp.einsum(
        "ua,tuv,vb->tab", keep_rows, quads, keep_rows, precision=lax.Precision.HIGHEST
    )
    shifted = weight_part.astype(jnp.float32) - step_size * update.reshape(
        summed.shape[0], TILE * TILE
    )
    return shifted.astype(jnp.bfloat16)


def forward(inputs, new_tiles):
    row_tiles = inputs.shape[1] // TILE
    col_tiles = new_tiles.shape[0] // row_tiles
    blocks = inputs.reshape(inputs.shape[0], row_tiles, TILE)
    matrix = new_tiles.reshape(row_tiles, col_tiles, TILE, TILE)
    output = jnp.einsum("tra,rcab->tcb", blocks, matrix, preferred_element_type=jnp.float32)
    return output.reshape(inputs.shape[0], col_tiles * TILE).astype(jnp.bfloat16)


def local(activations, cotangent, next_inputs, weight_tiles, momentum, chosen, counts):
    highest = lax.Precision.HIGHEST
    shards = lax.axis_size("tok")
    tiles_here = weight_tiles.shape[0]
    row_tiles = activations.shape[1] // TILE
    col_tiles = cotangent.shape[1] // TILE
    grad_scale = 1.0 / math.sqrt(activations.shape[0] * shards)
    keep_rows = cosine_rows(KEEP)
    row_span = min(tiles_here * lax.axis_size("tok") // col_tiles + 2, row_tiles)
    product = (
        lax.dot_general(
            activations, cotangent, (((0,), (0,)), ((), ())), preferred_element_type=jnp.float32
        )
        * grad_scale
    )
    tiled = product.reshape(row_span, TILE, col_tiles, TILE).transpose(0, 2, 1, 3)
    tiled = tiled.reshape(row_span * col_tiles, TILE * TILE)
    gradient = lax.psum_scatter(
        tiled.astype(jnp.bfloat16), "tok", scatter_dimension=0, tiled=True
    ).astype(jnp.float32)
    updated = momentum_decay * momentum[0] + gradient
    chosen_here = chosen[0, 0]
    in_list = jnp.arange(chosen_here.shape[0], dtype=jnp.int32) < counts[0, 0]
    picked = jnp.take(updated, chosen_here, axis=0).reshape(-1, TILE, TILE)
    quadrant = jnp.einsum("ua,nab,vb->nuv", keep_rows, picked, keep_rows, precision=highest)
    quadrant = jnp.where(in_list[:, None, None], quadrant, 0.0).astype(jnp.bfloat16)
    rebuilt = jnp.einsum(
        "ua,nuv,vb->nab", keep_rows, quadrant.astype(jnp.float32), keep_rows, precision=highest
    )
    new_momentum = updated.at[chosen_here].add(-rebuilt.reshape(-1, TILE * TILE))
    listed = jnp.where(in_list, chosen_here, -1)
    flat_quads = quadrant.reshape(-1, KEEP * KEEP)
    tile_numbers = jnp.arange(tiles_here, dtype=jnp.int32)
    all_quads, all_listed = (
        lax.all_gather(flat_quads, "replica", axis=0, tiled=True),
        lax.all_gather(listed, "replica", axis=0, tiled=True),
    )
    one_hot = (all_listed[:, None] == tile_numbers[None, :]).astype(jnp.bfloat16)
    summed = lax.dot_general(
        one_hot, all_quads, (((0,), (0,)), ((), ())), preferred_element_type=jnp.float32
    )
    new_part = rebuild(summed, weight_tiles, keep_rows)
    new_full = lax.all_gather(new_part, "tok", axis=0, tiled=True)
    values = forward(next_inputs, new_full)
    return (values, new_momentum[None])


def solution(mesh):
    return jax.shard_map(
        local,
        mesh=mesh,
        in_specs=(
            P(("replica", "tok"), None),
            P(("replica", "tok"), None),
            P(("replica", "tok"), None),
            P("tok", None),
            P("replica", "tok", None),
            P("replica", "tok", None),
            P("replica", "tok"),
        ),
        out_specs=(P(("replica", "tok"), None), P("replica", "tok", None)),
        check_vma=False,
    )
```

profile of v0, /device:TPU:0, one launch (start us, length us, event | category | flops | bytes accessed | tf_op | source)
XLA Modules:
  0.0 222.4 jit_solution(13789088672530609271)
XLA Ops:
  7.2 0.0 copy-start
  7.2 0.0 all-gather.3.cloned.1.call-start
  7.2 1.3 copy-done
  8.5 3.5 %multiply_convert_fusion = bf16[2880,512]{1,0:T(8,128)(2,1)} fusion(bf16[256,2880]{0,1:T(8,128)(2,1)S(1)} %copy-done, bf16[256,512]{1,0:T(8,128)(2,1)} %param.8), kind=kOutput, calls=%fused_computation.2 | convolution fusion | flops 757923840 | bytes 4685824 | tf_op jit(solution)/shard_map/dot_general | solution.py:54
  12.1 8.4 %convert_element_type.37 = bf16[45,64,8,64]{3,2,1,0:T(8,128)(2,1)} reshape(bf16[2880,512]{1,0:T(8,128)(2,1)} %multiply_convert_fusion) | data formatting | bytes 5898240 | tf_op jit(solution)/shard_map/convert_element_type | solution.py:62
  20.5 7.0 %copy.22 = bf16[45,8,64,64]{3,2,1,0:T(8,128)(2,1)} copy(bf16[45,8,64,64]{3,1,2,0:T(8,128)(2,1)} %bitcast.59) | data formatting | bytes 5898240 | tf_op jit(solution)/shard_map/convert_element_type | solution.py:62
  27.5 8.7 %convert_element_type.39 = bf16[360,4096]{1,0:T(8,128)(2,1)} reshape(bf16[45,8,64,64]{3,2,1,0:T(8,128)(2,1)} %copy.22) | data formatting | bytes 5898240 | tf_op jit(solution)/shard_map/convert_element_type | solution.py:62
  36.2 0.0 copy-start.3
  36.2 0.0 copy-start.4
  36.2 0.0 copy-start.2
  36.2 61.9 %fusion = bf16[96,4096]{1,0:T(8,128)(2,1)S(1)} fusion(bf16[360,4096]{1,0:T(8,128)(2,1)} %convert_element_type.39), kind=kCustom, calls=%all-reduce-scatter | all-reduce-scatter fusion | flops 1572865 | bytes 3736064
  98.2 1.7 collective-permute-start
  99.9 0.0 copy-done.3
  100.6 0.0 copy-done.4
  100.6 0.6 dynamic-slice
  101.9 0.1 fusion.39
  102.0 0.0 copy-done.2
  102.0 0.6 dynamic-slice.5
  103.2 8.0 %all-reduce = s32[64]{0:T(128)S(1)} all-reduce(s32[64]{0:T(128)S(1)} %fusion.39), channel_id=1, replica_groups=mesh['replica'=8,'tok'=4] {'replica'}, use_global_device_ids=true, to_apply=%add | all-reduce | flops 64 | bytes 512
  111.2 0.0 collective-permute-done
  111.3 5.8 %concatenate = bf16[114,4096]{1,0:T(8,128)(2,1)} concatenate(bf16[18,4096]{1,0:T(8,128)(2,1)S(1)} %collective-permute-done, bf16[96,4096]{1,0:T(8,128)(2,1)S(1)} %fusion), dimensions={0} | concatenate | bytes 1867776
  117.1 2.9 %bitcast_add_fusion = f32[90,4096]{1,0:T(8,128)S(1)} fusion(f32[1,90,4096]{2,0,1:T(1,128)} %param.11, bf16[114,4096]{1,0:T(8,128)(2,1)} %concatenate, u32[]{:S(6)} %subtract), kind=kLoop, calls=%fused_computation.4 | loop fusion | flops 1105920 | bytes 3686404 | tf_op jit(solution)/shard_map/add | solution.py:64
  119.9 0.6 gather_fusion
  120.5 0.1 gather.7
  120.6 0.4 fusion.7
  121.0 0.3 fusion.2
  121.3 0.1 reshape.90
  121.5 8.7 %all_gather.10 = bf16[64,1024]{1,0:T(8,128)(2,1)S(1)} all-gather(bf16[8,1024]{1,0:T(8,128)(2,1)S(1)} %reshape.90), channel_id=1, replica_groups=mesh['replica'=8,'tok'=4] {'replica'}, dimensions={0}, use_global_device_ids=true | all-gather | bytes 147456 | tf_op jit(solution)/shard_map/all_gather | solution.py:78
  130.2 0.3 fusion.11
  130.5 1.4 fusion.5
  131.9 3.9 %convolution_multiply_fusion = f32[90,64,64]{0,2,1:T(8,128)} fusion(f32[90,32,64]{0,2,1:T(8,128)S(1)} %fusion.5, f32[32]{0:T(128)S(1)} %compare_select_fusion.2, f32[64]{0:T(128)S(1)} %add_multiply_fusion), kind=kOutput, calls=%fused_computation.3 | convolution fusion | flops 141932544 | bytes 2212224 | tf_op jit(solution)/shard_map/ua,tuv,vb->tab/dot_general | solution.py:26
  135.8 2.8 %copy.26 = f32[90,4096]{1,0:T(8,128)} copy(f32[90,4096]{0,1:T(8,128)} %bitcast.61) | data formatting | bytes 2949120 | tf_op jit(solution)/shard_map/mul | solution.py:29
  138.6 2.6 %fusion.4 = bf16[1,90,4096]{2,1,0:T(8,128)(2,1)} fusion(f32[90,4096]{1,0:T(8,128)} %copy.26, bf16[90,4096]{1,0:T(8,128)(2,1)} %param.10), kind=kLoop, calls=%fused_computation.13 | loop fusion | flops 1105920 | bytes 2949120
  141.2 0.0 all-gather.3.cloned.1.call-update
  141.3 0.3 fusion.13
  141.6 0.6 convolution_negate_fusion
  142.2 0.1 reshape.106
  142.3 1.3 scatter_fusion
  143.7 2.6 %copy.30 = f32[1,90,4096]{2,0,1:T(1,128)} copy(f32[1,90,4096]{2,1,0:T(8,128)S(1)} %bitcast.60) | data formatting | bytes 2949120
  146.3 0.0 copy-start.1
  146.3 55.8 %all-gather.3.cloned.1.call-done = bf16[4,90,4096]{2,1,0:T(8,128)(2,1)} async-done(((bf16[1,90,4096]{2,1,0:T(8,128)(2,1)}), bf16[4,90,4096]{2,1,0:T(8,128)(2,1)}) %all-gather.3.cloned.1.call-update) | async-done | bytes 2949136 | tf_op jit(solution)/shard_map/all_gather | solution.py:86
  202.1 8.2 %reshape.92 = bf16[45,8,64,64]{3,2,1,0:T(8,128)(2,1)} reshape(bf16[4,90,4096]{2,1,0:T(8,128)(2,1)} %all-gather.3.cloned.1.call-done) | data formatting | bytes 5898240 | tf_op jit(solution)/shard_map/reshape | solution.py:39
  210.2 0.0 copy-done.1
  210.2 4.4 %fusion.1 = bf16[8,64,256]{2,1,0:T(8,128)(2,1)S(1)} fusion(bf16[45,8,64,64]{3,2,1,0:T(8,128)(2,1)} %reshape.92, bf16[256,45,64,1]{0,2,3,1:T(8,128)(2,1)S(1)} %bitcast.63), kind=kOutput, calls=%fused_computation.8 | convolution fusion | flops 755105792 | bytes 4685824 | tf_op jit(solution)/shard_map/tra,rcab->tcb/dot_general | solution.py:40
  214.7 0.8 copy.29
  (8 shorter events, 0.1 us)
Async XLA Ops:
  7.2 1.4 copy-start
  7.2 194.9 %all-gather.3.cloned.1.call-start = ((), (), s32[]{:S(2)}) async-start(), calls=%async_computation | async-start | bytes 3932160 | tf_op jit(solution)/shard_map/all_gather | solution.py:86
  36.2 63.7 %copy-start.3 = (s32[1,1,8]{2,1,0:T(1,128)S(1)}, s32[1,1,8]{2,1,0:T(1,128)}, u32[]{:S(2)}) copy-start(s32[1,1,8]{2,1,0:T(1,128)} %param.12) | copy-start | bytes 100
  36.2 64.4 %copy-start.4 = (u32[32]{0:T(128)S(1)}, u32[32]{0:T(128)}, u32[]{:S(2)}) copy-start(u32[32]{0:T(128)} %constant.48) | copy-start | bytes 388
  36.2 65.8 %copy-start.2 = (u32[32]{0:T(128)S(1)}, u32[32]{0:T(128)}, u32[]{:S(2)}) copy-start(u32[32]{0:T(128)} %constant.54) | copy-start | bytes 388
  98.2 13.1 %collective-permute-start = (bf16[18,4096]{1,0:T(8,128)(2,1)S(1)}, bf16[18,4096]{1,0:T(8,128)(2,1)S(1)}, u32[]{:S(2)}, u32[]{:S(2)}) collective-permute-start(bf16[18,4096]{1,0:T(8,128)(2,1)S(1)} %slice.2), channel_id=1, source_target_pairs={{0,1},{1,2},{2,3},{4,5},{5,6},{6,7},{8,9},{9,10},{10,11},{12,13},{... | collective-permute-start | bytes 442376
  146.3 64.0 %copy-start.1 = (bf16[256,2880]{0,1:T(8,128)(2,1)S(1)}, bf16[256,2880]{0,1:T(8,128)(2,1)}, u32[]{:S(2)}) copy-start(bf16[256,2880]{0,1:T(8,128)(2,1)} %param.9) | copy-start | bytes 4423684
Sparse Core Ops, SparseCore 0:
  141.4 60.6 all-gather.2
where the time goes:
time: 224 us; the launch traced here: 222 us
  blocking collectives  78.7 us (35%)
  waiting for transfers between devices  55.8 us (25%)
  local copies, waits for them, and re-layouts  47.9 us (21%)
  between operations  16.2 us (7%)
  matrix products  15.1 us (7%)
  other arithmetic  6.99 us (3%)
    unnamed x2, blocking collectives  69.9 us
    all_gather x1, waiting for transfers between devices, local(): new_full = lax.all_gather(new_part, 'tok', axis=0, tiled=True)  55.8 us
    convert_element_type x3, local copies, waits for them, and re-layouts, local(): tiled.astype(jnp.bfloat16)  24.1 us
    unnamed x17, local copies, waits for them, and re-layouts  11.9 us
    all_gather x1, blocking collectives, local(): lax.all_gather(flat_quads, 'replica', axis=0, tiled=True)  8.73 us
    reshape x1, local copies, waits for them, and re-layouts, forward(): matrix = new_tiles.reshape(row_tiles, col_tiles, TILE, TILE)  8.17 us
    dot_general x2, matrix products, rebuild(): jnp.einsum('ua,tuv,vb->tab', keep_rows, quads, keep_rows, precision=lax.P...  5.25 us
  transfers between devices with their start and end apart: 2, of which 1 were waited for; matrix products, arithmetic and copies ran while one was open for 3% of the time, Pallas kernels for 0%

commit v1 on v0

--- a/solution.py
+++ b/solution.py
@@ -1,16 +1,23 @@
+import functools
 import math
 
 import jax
 import jax.numpy as jnp
+import numpy as np
 from jax import lax
+from jax.experimental import pallas as pl
+from jax.experimental.pallas import tpu as pltpu
 from jax.sharding import PartitionSpec as P
 
 TILE = 64
 KEEP = 32
+LANES = 128
 
 
 momentum_decay = 0.9
 step_size = 0.01
+
+HIGHEST = lax.Precision.HIGHEST
 
 
 def cosine_rows(count):
@@ -23,9 +30,7 @@
 
 def rebuild(summed, weight_part, keep_rows):
     quads = summed.reshape(summed.shape[0], KEEP, KEEP)
-    update = jnp.einsum(
-        "ua,tuv,vb->tab", keep_rows, quads, keep_rows, precision=lax.Precision.HIGHEST
-    )
+    update = jnp.einsum("ua,tuv,vb->tab", keep_rows, quads, keep_rows, precision=HIGHEST)
     shifted = weight_part.astype(jnp.float32) - step_size * update.reshape(
         summed.shape[0], TILE * TILE
     )
@@ -41,23 +46,21 @@
     return output.reshape(inputs.shape[0], col_tiles * TILE).astype(jnp.bfloat16)
 
 
-def local(activations, cotangent, next_inputs, weight_tiles, momentum, chosen, counts):
-    highest = lax.Precision.HIGHEST
+def general(activations, cotangent, next_inputs, weight_tiles, momentum, chosen, counts):
     shards = lax.axis_size("tok")
     tiles_here = weight_tiles.shape[0]
     row_tiles = activations.shape[1] // TILE
     col_tiles = cotangent.shape[1] // TILE
     grad_scale = 1.0 / math.sqrt(activations.shape[0] * shards)
     keep_rows = cosine_rows(KEEP)
-    row_span = min(tiles_here * lax.axis_size("tok") // col_tiles + 2, row_tiles)
     product = (
         lax.dot_general(
             activations, cotangent, (((0,), (0,)), ((), ())), preferred_element_type=jnp.float32
         )
         * grad_scale
     )
-    tiled = product.reshape(row_span, TILE, col_tiles, TILE).transpose(0, 2, 1, 3)
-    tiled = tiled.reshape(row_span * col_tiles, TILE * TILE)
+    tiled = product.reshape(row_tiles, TILE, col_tiles, TILE).transpose(0, 2, 1, 3)
+    tiled = tiled.reshape(row_tiles * col_tiles, TILE * TILE)
     gradient = lax.psum_scatter(
         tiled.astype(jnp.bfloat16), "tok", scatter_dimension=0, tiled=True
     ).astype(jnp.float32)
@@ -65,10 +68,10 @@
     chosen_here = chosen[0, 0]
     in_list = jnp.arange(chosen_here.shape[0], dtype=jnp.int32) < counts[0, 0]
     picked = jnp.take(updated, chosen_here, axis=0).reshape(-1, TILE, TILE)
-    quadrant = jnp.einsum("ua,nab,vb->nuv", keep_rows, picked, keep_rows, precision=highest)
+    quadrant = jnp.einsum("ua,nab,vb->nuv", keep_rows, picked, keep_rows, precision=HIGHEST)
     quadrant = jnp.where(in_list[:, None, None], quadrant, 0.0).astype(jnp.bfloat16)
     rebuilt = jnp.einsum(
-        "ua,nuv,vb->nab", keep_rows, quadrant.astype(jnp.float32), keep_rows, precision=highest
+        "ua,nuv,vb->nab", keep_rows, quadrant.astype(jnp.float32), keep_rows, precision=HIGHEST
     )
     new_momentum = updated.at[chosen_here].add(-rebuilt.reshape(-1, TILE * TILE))
     listed = jnp.where(in_list, chosen_here, -1)
@@ -86,6 +89,391 @@
     new_full = lax.all_gather(new_part, "tok", axis=0, tiled=True)
     values = forward(next_inputs, new_full)
     return (values, new_momentum[None])
+
+
+def low_rows():
+    u = np.arange(KEEP)[:, None].astype(np.float64)
+    i = np.arange(TILE)[None, :].astype(np.float64)
+    factor = np.where(u == 0, math.sqrt(1.0 / TILE), math.sqrt(2.0 / TILE))
+    return np.cos(math.pi * (2 * i + 1) * u / (2 * TILE)) * factor
+
+
+def tables():
+    low = low_rows()
+    split = np.concatenate([low[:, 0::2], low[:, 1::2]], axis=0)
+    into = np.zeros((4 * LANES, LANES))
+    back = np.zeros((LANES, 4 * LANES))
+    for g in range(4):
+        into[g * LANES : g * LANES + TILE, g * KEEP : (g + 1) * KEEP] = low.T
+        for half in range(2):
+            at = g * LANES + half * TILE
+            back[g * KEEP : (g + 1) * KEEP, at : at + TILE] = low
+    split_back = np.concatenate([low[:, 0::2].T, low[:, 1::2].T], axis=0)
+    return [t.astype(np.float32) for t in (split, into, split_back, back)]
+
+
+def lane_index(shape):
+    return lax.broadcasted_iota(jnp.int32, shape, len(shape) - 1)
+
+
+def tile_products(start, act_ref, cot_ref, sent_ref, cot_row, grid_ref, tiled_ref, scale, spans):
+    tokens = act_ref.shape[1]
+    width = cot_ref.shape[1]
+    first_half = lane_index((KEEP, LANES)) < TILE
+    step = 2 * TILE
+    theirs = [
+        sent_ref[0][cot_row + n * tokens : cot_row + (n + 1) * tokens, :]
+        for n in range(width // tokens)
+    ]
+    for block in range(spans // 2):
+        rows = pl.ds(pl.multiple_of(start + block * step, TILE), step)
+        mine = jnp.dot(act_ref[rows, :], cot_ref[...], preferred_element_type=jnp.float32)
+        other = sent_ref[1][block * step : (block + 1) * step, :]
+        for n, piece in enumerate(theirs):
+            lanes = slice(n * tokens, (n + 1) * tokens)
+            theirs_here = jnp.dot(other, piece, preferred_element_type=jnp.float32)
+            both = (mine[:, lanes] + theirs_here) * scale
+            for m in range(tokens // LANES):
+                grid_ref[n * (tokens // LANES) + m] = both[:, m * LANES : (m + 1) * LANES]
+        for half in range(2):
+            for m in range(width // LANES):
+                even = grid_ref[m, pl.ds(half * TILE, KEEP, stride=2), :]
+                odd = grid_ref[m, pl.ds(half * TILE + 1, KEEP, stride=2), :]
+                tile = (2 * block + half) * (width // TILE) + 2 * m
+                tiled_ref[tile * KEEP : (tile + 1) * KEEP, :] = jnp.where(
+                    first_half, even, pltpu.roll(odd, TILE, 1)
+                )
+                tiled_ref[(tile + 1) * KEEP : (tile + 2) * KEEP, :] = jnp.where(
+                    first_half, pltpu.roll(even, TILE, 1), odd
+                )
+
+
+def to_low(picked, split_ref, into_ref):
+    wide = jnp.concatenate(picked, axis=1)
+    mixed = jnp.dot(split_ref[...], wide, precision=HIGHEST, preferred_element_type=jnp.float32)
+    out = []
+    for h in range(len(picked) // 4):
+        pieces = []
+        for g in range(4):
+            lanes = slice((4 * h + g) * LANES, (4 * h + g + 1) * LANES)
+            pieces.append(mixed[:KEEP, lanes] + pltpu.roll(mixed[KEEP:, lanes], TILE, 1))
+        row = jnp.concatenate(pieces, axis=1)
+        out.append(
+            jnp.dot(row, into_ref[...], precision=HIGHEST, preferred_element_type=jnp.float32)
+        )
+    return out
+
+
+def far_kernel(
+    at_ref, chosen_ref, act_ref, cot_ref, sent_ref, split_ref, into_ref,
+    sum_ref, low_ref, grid_ref, tiled_ref, *, scale, spans,
+):
+    start, skip = at_ref[0], at_ref[1]
+    tile_products(
+        start, act_ref, cot_ref, (sent_ref, sent_ref), spans * TILE, grid_ref, tiled_ref, scale,
+        spans,
+    )
+    slots = chosen_ref.shape[0]
+    picked = [
+        tiled_ref[pl.ds(pl.multiple_of((skip + chosen_ref[s]) * KEEP, KEEP), KEEP), :]
+        for s in range(slots)
+    ]
+    for h, part in enumerate(to_low(picked, split_ref, into_ref)):
+        low_ref[h * KEEP : (h + 1) * KEEP, :] = part
+    rows = sum_ref.shape[0]
+    chunk = 10 * KEEP
+    for c in range(0, rows, chunk):
+        sum_ref[c : c + chunk, :] = tiled_ref[
+            pl.ds(pl.multiple_of(skip * KEEP + c, KEEP), chunk), :
+        ].astype(jnp.bfloat16)
+
+
+def own_kernel(
+    at_ref, chosen_ref, act_ref, cot_ref, sent_ref, near_ref, mom_ref, far_low_ref,
+    split_ref, into_ref, split_back_ref, back_ref,
+    base_ref, quad_ref, grid_ref, tiled_ref, *, scale, spans,
+):
+    start, skip, count = at_ref[0], at_ref[1], at_ref[2]
+    tile_products(
+        start, act_ref, cot_ref, (sent_ref, near_ref), spans * TILE, grid_ref, tiled_ref, scale,
+        spans,
+    )
+    rows = base_ref.shape[0]
+    chunk = 10 * KEEP
+    for c in range(0, rows, chunk):
+        base_ref[c : c + chunk, :] = (
+            momentum_decay * mom_ref[c : c + chunk, :]
+            + tiled_ref[pl.ds(pl.multiple_of(skip * KEEP + c, KEEP), chunk), :]
+        )
+    slots = chosen_ref.shape[0]
+    places = [
+        pl.ds(pl.multiple_of(chosen_ref[s] * KEEP, KEEP), KEEP) for s in range(slots)
+    ]
+    lows = to_low([base_ref[place, :] for place in places], split_ref, into_ref)
+    group = lane_index((KEEP, LANES)) // KEEP
+    first_half = lax.rem(lane_index((KEEP, 4 * LANES)), LANES) < TILE
+    for h, low in enumerate(lows):
+        low = low + far_low_ref[h * KEEP : (h + 1) * KEEP, :]
+        quad = jnp.where(group + 4 * h < count, low, 0.0).astype(jnp.bfloat16)
+        quad_ref[h * KEEP : (h + 1) * KEEP, :] = quad
+        wide = jnp.dot(
+            quad.astype(jnp.float32), back_ref[...], precision=HIGHEST,
+            preferred_element_type=jnp.float32,
+        )
+        both = jnp.dot(
+            split_back_ref[...], wide, precision=HIGHEST, preferred_element_type=jnp.float32
+        )
+        rebuilt = jnp.where(first_half, both[:KEEP, :], both[KEEP:, :])
+        for g in range(4):
+            place = places[4 * h + g]
+            base_ref[place, :] = base_ref[place, :] - rebuilt[:, g * LANES : (g + 1) * LANES]
+
+
+def lows_kernel(inputs_ref, high_ref, low_ref, out_ref, lows_ref, *, span):
+    rows = inputs_ref.shape[0]
+    half = span // 2
+    lows_ref[...] = jnp.zeros_like(lows_ref)
+    for c in range(rows // span):
+        piece = inputs_ref[c * span : (c + 1) * span, :]
+        lows_ref[c * half : (c + 1) * half, :] = jnp.dot(
+            high_ref[...], piece, preferred_element_type=jnp.float32
+        ) + jnp.dot(low_ref[...], piece, preferred_element_type=jnp.float32)
+    out_ref[...] = lows_ref[...].T.astype(jnp.bfloat16)
+
+
+def last_kernel(tiles_ref, quads_ref, lows_ref, base_ref, high_ref, low_ref, out_ref, sum_ref,
+                *, slots, col_tiles):
+    sum_ref[...] = jnp.zeros_like(sum_ref)
+    group = lane_index((KEEP, LANES)) // KEEP
+    held = (slots // 4) * KEEP
+
+    def add_list(n, carry):
+        puts = []
+        for s in range(slots):
+            tile = tiles_ref[n * slots + s]
+            i, j = tile // col_tiles, lax.rem(tile, col_tiles)
+            h, g = s // 4, s % 4
+            at = pl.ds(pl.multiple_of(n * held + h * KEEP, KEEP), KEEP)
+            quad = quads_ref[at, :].astype(jnp.float32)
+            to = lax.rem(j, 4)
+            moved = pltpu.roll(quad, lax.rem(to - g + 4, 4) * KEEP, 1)
+            place = sum_ref.at[j // 4, pl.ds(pl.multiple_of(i * KEEP, KEEP), KEEP)]
+            puts.append((place, place[...] + moved, group == to))
+        for place, value, mask in puts:
+            pltpu.store(place, value, mask=mask)
+        return carry
+
+    lax.fori_loop(0, quads_ref.shape[0] // held, add_list, 0)
+    parts = []
+    for half in range(sum_ref.shape[0]):
+        whole = sum_ref[half]
+        top = whole.astype(jnp.bfloat16)
+        rest = (whole - top.astype(jnp.float32)).astype(jnp.bfloat16)
+        parts.append(
+            jnp.dot(lows_ref[...], top, preferred_element_type=jnp.float32)
+            + jnp.dot(lows_ref[...], rest, preferred_element_type=jnp.float32)
+        )
+    mixed = jnp.concatenate(parts, axis=1)
+    top = mixed.astype(jnp.bfloat16)
+    rest = (mixed - top.astype(jnp.float32)).astype(jnp.bfloat16)
+    update = (
+        jnp.dot(top, high_ref[...], preferred_element_type=jnp.float32)
+        + jnp.dot(rest, high_ref[...], preferred_element_type=jnp.float32)
+        + jnp.dot(top, low_ref[...], preferred_element_type=jnp.float32)
+    )
+    out_ref[...] = (base_ref[...] - step_size * update).astype(jnp.bfloat16)
+
+
+def split_bf16(table):
+    top = table.astype(jnp.bfloat16)
+    return top, (table - top.astype(np.float32)).astype(jnp.bfloat16)
+
+
+def vmem(count):
+    return [pl.BlockSpec(memory_space=pltpu.VMEM)] * count
+
+
+def smem(count):
+    return [pl.BlockSpec(memory_space=pltpu.SMEM)] * count
+
+
+def swap(array, axis, bit):
+    size = lax.axis_size(axis)
+    return lax.ppermute(array, axis, [(i, i ^ bit) for i in range(size)])
+
+
+def doubled(array, axis, bit):
+    return jnp.concatenate([array, swap(array, axis, bit)], axis=0)
+
+
+def fits(shards, replicas, activations, cotangent, weight_tiles, slots):
+    tokens, depth = activations.shape
+    width = cotangent.shape[1]
+    tiles_here = weight_tiles.shape[0]
+    span = span_of(tiles_here, width // TILE)
+    return (
+        shards == 4
+        and replicas == 8
+        and tokens % LANES == 0
+        and width % tokens == 0
+        and width // TILE == 8
+        and slots % 4 == 0
+        and depth % (5 * TILE) == 0
+        and tiles_here % 10 == 0
+        and tiles_here <= 256
+        and slots <= 128
+        and span % 2 == 0
+        and all((n * tiles_here) // 8 + span <= depth // TILE for n in range(shards))
+        and all((n * tiles_here) % 8 + tiles_here <= span * 8 for n in range(shards))
+    )
+
+
+def span_of(tiles_here, col_tiles):
+    return 2 * (-(-tiles_here // col_tiles) // 2)
+
+
+def local(activations, cotangent, next_inputs, weight_tiles, momentum, chosen, counts):
+    shards = lax.axis_size("tok")
+    replicas = lax.axis_size("replica")
+    slots = chosen.shape[-1]
+    if not fits(shards, replicas, activations, cotangent, weight_tiles, slots):
+        return general(
+            activations, cotangent, next_inputs, weight_tiles, momentum, chosen, counts
+        )
+    tokens, depth = activations.shape
+    width = cotangent.shape[1]
+    tiles_here = weight_tiles.shape[0]
+    row_tiles = depth // TILE
+    col_tiles = width // TILE
+    spans = span_of(tiles_here, col_tiles)
+    span_rows = spans * TILE
+    scale = 1.0 / math.sqrt(tokens * shards)
+    me = lax.axis_index("tok")
+    rep = lax.axis_index("replica")
+    act = activations.T
+    inputs = next_inputs.T
+    split, into, split_back, back = tables()
+
+    def start_of(shard):
+        return (shard * tiles_here) // col_tiles * TILE
+
+    def skip_of(shard):
+        return lax.rem(shard * tiles_here, col_tiles)
+
+    def rows_for(shard):
+        return lax.dynamic_slice(act, (start_of(shard), 0), (span_rows, tokens))
+
+    share = TILE * TILE // replicas
+    listed = chosen[0, 0].astype(jnp.bfloat16)
+    pad_rows = -(tiles_here + 1) % 8 + 1
+    piece = jnp.concatenate(
+        [
+            lax.dynamic_slice(weight_tiles, (0, rep * share), (tiles_here, share)),
+            jnp.zeros((pad_rows, share), jnp.bfloat16).at[0, :slots].set(listed),
+        ],
+        axis=0,
+    )[None]
+
+    cot_parts = [cotangent[:, n * tokens : (n + 1) * tokens] for n in range(width // tokens)]
+    sent_far = swap(jnp.concatenate([rows_for(me ^ 3), *cot_parts], axis=0), "tok", 1)
+    pieces = doubled(doubled(piece, "tok", 1), "tok", 2)
+    sent_near = swap(rows_for(me ^ 1), "tok", 1)
+
+    lists = pieces[:, tiles_here, :slots]
+    far = me ^ 2
+    far_chosen = lists[2].astype(jnp.int32)
+    grid_scratch = [
+        pltpu.VMEM((width // LANES, 2 * TILE, LANES), jnp.float32),
+        pltpu.VMEM((spans * col_tiles * KEEP, LANES), jnp.float32),
+    ]
+    far_sum, far_low = pl.pallas_call(
+        functools.partial(far_kernel, scale=scale, spans=spans),
+        out_shape=(
+            jax.ShapeDtypeStruct((tiles_here * KEEP, LANES), jnp.bfloat16),
+            jax.ShapeDtypeStruct((slots // 4 * KEEP, LANES), jnp.float32),
+        ),
+        in_specs=smem(2) + vmem(5),
+        out_specs=tuple(vmem(2)),
+        scratch_shapes=grid_scratch,
+        name="far",
+    )(
+        jnp.stack([start_of(far), skip_of(far)]), far_chosen, act, cotangent, sent_far,
+        split, into,
+    )
+    low_from = swap(far_low, "tok", 2)
+    sum_from = swap(far_sum, "tok", 2)
+
+    moment = momentum.reshape(tiles_here * KEEP, LANES)
+    base, quads = pl.pallas_call(
+        functools.partial(own_kernel, scale=scale, spans=spans),
+        out_shape=(
+            jax.ShapeDtypeStruct((tiles_here * KEEP, LANES), jnp.float32),
+            jax.ShapeDtypeStruct((slots // 4 * KEEP, LANES), jnp.bfloat16),
+        ),
+        in_specs=smem(2) + vmem(10),
+        out_specs=tuple(vmem(2)),
+        scratch_shapes=grid_scratch,
+        name="own",
+    )(
+        jnp.stack([start_of(me), skip_of(me), counts[0, 0]]), chosen[0, 0], act, cotangent,
+        sent_far, sent_near, moment, low_from, split, into, split_back, back,
+    )
+    new_momentum = (base + sum_from.astype(jnp.float32)).reshape(momentum.shape)
+
+    shard_order = [lax.dynamic_index_in_dim(pieces, me ^ n, 0, False) for n in range(shards)]
+    whole = jnp.concatenate([p[:tiles_here] for p in shard_order], axis=0)
+    rows_share = TILE // replicas
+    matrix = whole.reshape(row_tiles, col_tiles, rows_share, TILE).transpose(0, 2, 1, 3)
+    matrix = matrix.reshape(row_tiles * rows_share, width)
+    list_rows = jnp.zeros((8, width), jnp.bfloat16).at[:shards, :slots].set(lists)
+    held = jnp.concatenate([matrix, list_rows], axis=0)[None]
+    for bit in (2, 4, 1):
+        held = doubled(held, "replica", bit)
+    all_lists = held[:, matrix.shape[0] : matrix.shape[0] + shards, :slots].astype(jnp.int32)
+    owners = me ^ jnp.arange(shards, dtype=jnp.int32)
+    all_tiles = (all_lists + (owners * tiles_here)[None, :, None]).reshape(-1)
+    order = [n1 * 1 ^ n2 * 4 ^ n3 * 2 for n1 in range(2) for n2 in range(2) for n3 in range(2)]
+    by_share = inputs.reshape(row_tiles, replicas, rows_share, tokens)
+    mine = jnp.concatenate(
+        [
+            lax.dynamic_index_in_dim(by_share, rep ^ o, 1, False).reshape(-1, tokens)
+            for o in order
+        ],
+        axis=0,
+    )
+    kept = held[:, : matrix.shape[0]].reshape(depth, width)
+    unchanged = lax.dot_general(
+        mine, kept, (((0,), (0,)), ((), ())), preferred_element_type=jnp.float32
+    )
+
+    low = low_rows().astype(np.float32)
+    at_once = 5
+    along = np.kron(np.eye(at_once, dtype=np.float32), low)
+    along_high, along_low = split_bf16(along)
+    padded = -(-row_tiles * KEEP // LANES) * LANES
+    lows = pl.pallas_call(
+        functools.partial(lows_kernel, span=at_once * TILE),
+        out_shape=jax.ShapeDtypeStruct((tokens, padded), jnp.bfloat16),
+        in_specs=vmem(3),
+        out_specs=vmem(1)[0],
+        scratch_shapes=[pltpu.VMEM((padded, tokens), jnp.float32)],
+        name="lows",
+    )(inputs, along_high, along_low)
+
+    gathered = doubled(doubled(quads[None], "tok", 1), "tok", 2)
+    for bit in (2, 4, 1):
+        gathered = doubled(gathered, "replica", bit)
+    across = np.kron(np.eye(col_tiles, dtype=np.float32), low)
+    across_high, across_low = split_bf16(across)
+    values = pl.pallas_call(
+        functools.partial(last_kernel, slots=slots, col_tiles=col_tiles),
+        out_shape=jax.ShapeDtypeStruct((tokens, width), jnp.bfloat16),
+        in_specs=smem(1) + vmem(5),
+        out_specs=vmem(1)[0],
+        scratch_shapes=[pltpu.VMEM((col_tiles // 4, padded, LANES), jnp.float32)],
+        name="last",
+    )(all_tiles, gathered.reshape(-1, LANES), lows, unchanged, across_high, across_low)
+    return (values, new_momentum)
 
 
 def solution(mesh):

time: 224 us -> 133 us (0.59)
  blocking collectives: 78.7 us -> 0 us
  local copies, waits for them, and re-layouts: 47.9 us -> 20.9 us
  starting transfers between devices: 1.74 us -> 23.6 us
  Pallas kernels: 0 us -> 21.4 us
  between operations: 16.2 us -> 1.44 us
  matrix products: 15.1 us -> 1.82 us
  other arithmetic: 6.99 us -> 11.4 us
  waiting for transfers between devices: 55.8 us -> 51.7 us
    unnamed x2 -> x0, blocking collectives: 69.9 us -> none
    all_gather x1 -> x0, waiting for transfers between devices: 55.8 us -> none  [local(): new_full = lax.all_gather(new_part, 'tok', axis=0, tiled=True)]
    ppermute x0 -> x14, waiting for transfers between devices: none -> 51.7 us  [swap(): return lax.ppermute(array, axis, [(i, i ^ bit) for i in range(size)])]
    convert_element_type x3 -> x0, local copies, waits for them, and re-layouts: 24.1 us -> none  [local(): tiled.astype(jnp.bfloat16)]
    ppermute x0 -> x14, starting transfers between devices: none -> 23.6 us  [swap(): return lax.ppermute(array, axis, [(i, i ^ bit) for i in range(size)])]
    pallas_call x0 -> x4, Pallas kernels: none -> 21.4 us  [the longest x1 8.36 us: local(): pl.pallas_call(functools.partial(last_kernel, slots=slots, col_tiles=col_...]
    dot_general x9 -> x1, matrix products: 15.1 us -> 1.82 us  [local(): lax.dot_general(mine, kept, (((0,), (0,)), ((), ())), preferred_element_t...]
    all_gather x1 -> x0, blocking collectives: 8.73 us -> none  [local(): lax.all_gather(flat_quads, 'replica', axis=0, tiled=True)]
  transfers between devices with their start and end apart: 2 -> 14, of which waited for: 1 -> 5; matrix products, arithmetic and copies ran while one was open for 3% -> 21% of each run, Pallas kernels for 0% -> 10%
where the time goes in v1:
time: 133 us; the launch traced here: 132 us
  waiting for transfers between devices  51.7 us (39%)
  starting transfers between devices  23.6 us (18%)
  Pallas kernels  21.4 us (16%)
  local copies, waits for them, and re-layouts  20.9 us (16%)
  other arithmetic  11.4 us (9%)
  matrix products  1.82 us (1%)
  between operations  1.44 us (1%)
    ppermute x14, waiting for transfers between devices, swap(): return lax.ppermute(array, axis, [(i, i ^ bit) for i in range(size)])  51.7 us
    ppermute x14, starting transfers between devices, swap(): return lax.ppermute(array, axis, [(i, i ^ bit) for i in range(size)])  23.6 us
    unnamed x26, local copies, waits for them, and re-layouts  12.1 us
    pallas_call x1, Pallas kernels, local(): pl.pallas_call(functools.partial(last_kernel, slots=slots, col_tiles=col_...  8.36 us
    pallas_call x1, Pallas kernels, local(): pl.pallas_call(functools.partial(own_kernel, scale=scale, spans=spans), o...  5.93 us
    concatenate x8, other arithmetic, doubled(): return jnp.concatenate([array, swap(array, axis, bit)], axis=0)  4.92 us
    pallas_call x1, Pallas kernels, local(): pl.pallas_call(functools.partial(far_kernel, scale=scale, spans=spans), o...  3.72 us
    pallas_call x1, Pallas kernels, local(): pl.pallas_call(functools.partial(lows_kernel, span=at_once * TILE), out_s...  3.36 us
  transfers between devices with their start and end apart: 14, of which 5 were waited for; matrix products, arithmetic and copies ran while one was open for 21% of the time, Pallas kernels for 10%

profile of v1, /device:TPU:0, one launch (start us, length us, event | category | flops | bytes accessed | tf_op | source)
XLA Modules:
  0.0 132.2 jit_solution(14782864508456996296)
XLA Ops:
  0.6 0.0 copy-start
  0.7 0.7 convert_bitcast_fusion
  1.4 0.4 copy-done
  1.8 3.1 %collective-permute-start = (bf16[1,96,512]{2,1,0:T(8,128)(2,1)S(1)}, bf16[1,96,512]{2,1,0:T(8,128)(2,1)S(1)}, u32[]{:S(2)}, u32[]{:S(2)}) collective-permute-start(bf16[1,96,512]{2,1,0:T(8,128)(2,1)S(1)} %fusion.5), channel_id=1, source_target_pairs={{0,1},{1,0},{2,3},{3,2},{4,5},{5,4},{6,7},{7,6},{8,9},{9,8},{10,11... | collective-permute-start | bytes 294920 | tf_op jit(solution)/shard_map/ppermute | solution.py:302
  4.9 1.0 fusion.7
  5.9 0.0 copy-start.3
  5.9 2.0 %dynamic-slice_bitcast_fusion = (bf16[768,256]{1,0:T(8,128)(2,1)}, bf16[768,256]{1,0:T(8,128)(2,1)S(1)}) fusion(bf16[256,2880]{0,1:T(8,128)(2,1)} %param.19, s32[]{:T(128)S(6)} %select_n.70, s32[]{:T(128)S(6)} %select_n.68), kind=kLoop, calls=%fused_computation.11 | loop fusion | bytes 1572872 | tf_op jit(solution)/shard_map/dynamic_slice | solution.py:364
  8.0 0.9 pad_maximum_fusion.5
  8.9 0.1 collective-permute-start.5
  8.9 2.0 %collective-permute-start.6 = (bf16[768,256]{1,0:T(8,128)(2,1)}, bf16[768,256]{1,0:T(8,128)(2,1)}, u32[]{:S(2)}, u32[]{:S(2)}) collective-permute-start(bf16[768,256]{1,0:T(8,128)(2,1)} %get-tuple-element.38), channel_id=1, source_target_pairs={{0,1},{1,0},{2,3},{3,2},{4,5},{5,4},{6,7},{7,6},{8,9},{9,8},{10,11... | collective-permute-start | bytes 1179656 | tf_op jit(solution)/shard_map/ppermute | solution.py:302
  10.9 0.7 bitcast_dynamic-update-slice_fusion.7
  11.6 0.7 bitcast_dynamic-update-slice_fusion.6
  12.3 0.7 bitcast_dynamic-update-slice_fusion.5
  13.0 0.0 collective-permute-done
  13.0 2.7 %collective-permute-start.1 = (bf16[2,96,512]{2,1,0:T(8,128)(2,1)S(1)}, bf16[2,96,512]{2,1,0:T(8,128)(2,1)S(1)}, u32[]{:S(2)}, u32[]{:S(2)}) collective-permute-start(bf16[2,96,512]{2,1,0:T(8,128)(2,1)S(1)} %pad_maximum_fusion.8), channel_id=1, source_target_pairs={{0,2},{1,3},{2,0},{3,1},{4,6},{5,7},{6,4},{7,5},{8,10},{9,11},{10,... | collective-permute-start | bytes 589832 | tf_op jit(solution)/shard_map/ppermute | solution.py:302
  15.7 0.7 bitcast_dynamic-update-slice_fusion.4
  16.4 0.7 bitcast_dynamic-update-slice_fusion.3
  17.0 18.7 %collective-permute-done.1 = bf16[2,96,512]{2,1,0:T(8,128)(2,1)S(1)} collective-permute-done((bf16[2,96,512]{2,1,0:T(8,128)(2,1)S(1)}, bf16[2,96,512]{2,1,0:T(8,128)(2,1)S(1)}, u32[]{:S(2)}, u32[]{:S(2)}) %collective-permute-start.1) | collective-permute-done | bytes 196640 | tf_op jit(solution)/shard_map/ppermute | solution.py:302
  35.9 0.1 pad_maximum_fusion.7
  36.0 0.4 reshape.138
  36.3 0.1 copy.23
  36.5 0.4 reshape.139
  37.0 1.7 %collective-permute-start.2 = (bf16[1,368,512]{2,1,0:T(8,128)(2,1)S(1)}, bf16[1,368,512]{2,1,0:T(8,128)(2,1)S(1)}, u32[]{:S(2)}, u32[]{:S(2)}) collective-permute-start(bf16[1,368,512]{2,1,0:T(8,128)(2,1)S(1)} %fusion.2), channel_id=1, source_target_pairs={{0,8},{4,12},{8,0},{12,4},{16,24},{20,28},{24,16},{28,20},{1,9},{5... | collective-permute-start | bytes 1130504 | tf_op jit(solution)/shard_map/ppermute | solution.py:302
  38.6 0.7 pad_add_fusion.1.at_ref
  40.0 0.6 pad_add_fusion.at_ref
  40.6 0.5 fusion.6.chosen_ref
  41.1 0.0 collective-permute-done.5.sent_ref
  41.1 0.8 copy-done.4
  41.9 3.7 %far.1 = (bf16[2880,128]{1,0:T(8,128)(2,1)}, f32[64,128]{1,0:T(8,128)}) custom-call(s32[2]{0:T(128)} %pad_add_fusion.1.at_ref, s32[8]{0:T(128)} %fusion.6.chosen_ref, bf16[2880,256]{1,0:T(8,128)(2,1)} %bitcast.67, bf16[256,512]{1,0:T(8,128)(2,1)} %cot_ref.3, bf16[1280,256]{1,0:T(8,128)(2,1)} %copy-done.4, f32[64,32]{1,0:T(8,128)} %constant.163.clone.split_ref, ...), custom_call_target="tpu_custom_call" | custom-call | tf_op jit(solution)/shard_map/far/pallas_call | solution.py:389
  45.7 3.4 %collective-permute-start.7 = (f32[64,128]{1,0:T(8,128)}, f32[64,128]{1,0:T(8,128)S(1)}, u32[]{:S(2)}, u32[]{:S(2)}) collective-permute-start(f32[64,128]{1,0:T(8,128)} %get-tuple-element.30), channel_id=1, source_target_pairs={{0,2},{1,3},{2,0},{3,1},{4,6},{5,7},{6,4},{7,5},{8,10},{9,11},{10,... | collective-permute-start | bytes 98312 | tf_op jit(solution)/shard_map/ppermute | solution.py:302
  49.0 0.1 pad_maximum_fusion.4
  49.1 1.6 %collective-permute-start.3 = (bf16[2,368,512]{2,1,0:T(8,128)(2,1)S(1)}, bf16[2,368,512]{2,1,0:T(8,128)(2,1)S(1)}, u32[]{:S(2)}, u32[]{:S(2)}) collective-permute-start(bf16[2,368,512]{2,1,0:T(8,128)(2,1)S(1)} %pad_maximum_fusion.4), channel_id=1, source_target_pairs={{0,16},{4,20},{8,24},{12,28},{16,0},{20,4},{24,8},{28,12},{1,17},{... | collective-permute-start | bytes 2261000 | tf_op jit(solution)/shard_map/ppermute | solution.py:302
  50.7 0.4 collective-permute-done.7.far_low_ref
  51.1 0.6 copy-done.5
  51.8 5.9 %own.1 = (f32[2880,128]{1,0:T(8,128)}, bf16[64,128]{1,0:T(8,128)(2,1)}) custom-call(s32[3]{0:T(128)} %pad_add_fusion.at_ref, s32[8]{0:T(128)} %bitcast.87, bf16[2880,256]{1,0:T(8,128)(2,1)} %bitcast.68, bf16[256,512]{1,0:T(8,128)(2,1)} %cot_ref.3, bf16[1280,256]{1,0:T(8,128)(2,1)} %copy-done.4, bf16[768,256]{1,0:T(8,128)(2,1)} %collective-permute-done.6.near_ref, ...), custom_call_target="tpu_custom_call" | custom-call | tf_op jit(solution)/shard_map/own/pallas_call | solution.py:407
  57.7 4.2 %collective-permute-start.8 = (bf16[1,64,128]{2,1,0:T(8,128)(2,1)}, bf16[1,64,128]{2,1,0:T(8,128)(2,1)S(1)}, u32[]{:S(2)}, u32[]{:S(2)}) collective-permute-start(bf16[1,64,128]{2,1,0:T(8,128)(2,1)} %bitcast.82), channel_id=1, source_target_pairs={{0,1},{1,0},{2,3},{3,2},{4,5},{5,4},{6,7},{7,6},{8,9},{9,8},{10,11... | collective-permute-start | bytes 49160 | tf_op jit(solution)/shard_map/ppermute | solution.py:302
  61.9 1.6 %bitcast_dynamic-update-slice_fusion.2 = bf16[2880,256]{1,0:T(8,128)(2,1)} fusion(bf16[2880,256]{1,0:T(8,128)(2,1)} %bitcast_dynamic-update-slice_fusion.3, bf16[45,8,8,256]{3,2,1,0:T(8,128)(2,1)} %bitcast.69, s32[]{:T(128)S(6)} %select_n.77), kind=kLoop, calls=%fused_computation.21 | loop fusion | bytes 368644
  63.5 0.3 collective-permute-start.13
  63.8 0.7 pad_maximum_fusion.11
  64.6 2.6 %collective-permute-start.9 = (bf16[2,64,128]{2,1,0:T(8,128)(2,1)S(1)}, bf16[2,64,128]{2,1,0:T(8,128)(2,1)S(1)}, u32[]{:S(2)}, u32[]{:S(2)}) collective-permute-start(bf16[2,64,128]{2,1,0:T(8,128)(2,1)S(1)} %pad_maximum_fusion.11), channel_id=1, source_target_pairs={{0,2},{1,3},{2,0},{3,1},{4,6},{5,7},{6,4},{7,5},{8,10},{9,11},{10,... | collective-permute-start | bytes 98312 | tf_op jit(solution)/shard_map/ppermute | solution.py:302
  67.1 1.3 %constant_dynamic-update-slice_fusion.4 = (bf16[16,64,128]{2,1,0:T(8,128)(2,1)}, bf16[32,64,128]{2,1,0:T(8,128)(2,1)}) fusion(bf16[64,128]{1,0:T(8,128)(2,1)} %get-tuple-element.31), kind=kLoop, calls=%fused_computation.39 | loop fusion | bytes 49152
  68.5 28.6 %collective-permute-done.9 = bf16[2,64,128]{2,1,0:T(8,128)(2,1)S(1)} collective-permute-done((bf16[2,64,128]{2,1,0:T(8,128)(2,1)S(1)}, bf16[2,64,128]{2,1,0:T(8,128)(2,1)S(1)}, u32[]{:S(2)}, u32[]{:S(2)}) %collective-permute-start.9) | collective-permute-done | bytes 32800 | tf_op jit(solution)/shard_map/ppermute | solution.py:302
  97.0 0.7 pad_maximum_fusion.10
  97.7 0.5 collective-permute-start.10
  98.3 0.6 constant_dynamic-update-slice_fusion.3
  98.9 3.1 %collective-permute-done.10 = bf16[4,64,128]{2,1,0:T(8,128)(2,1)S(1)} collective-permute-done((bf16[4,64,128]{2,1,0:T(8,128)(2,1)S(1)}, bf16[4,64,128]{2,1,0:T(8,128)(2,1)S(1)}, u32[]{:S(2)}, u32[]{:S(2)}) %collective-permute-start.10) | collective-permute-done | bytes 65568 | tf_op jit(solution)/shard_map/ppermute | solution.py:302
  102.0 0.7 pad_maximum_fusion.9
  102.7 1.6 %collective-permute-start.11 = (bf16[8,64,128]{2,1,0:T(8,128)(2,1)S(1)}, bf16[8,64,128]{2,1,0:T(8,128)(2,1)S(1)}, u32[]{:S(2)}, u32[]{:S(2)}) collective-permute-start(bf16[8,64,128]{2,1,0:T(8,128)(2,1)S(1)} %pad_maximum_fusion.9), channel_id=1, source_target_pairs={{0,16},{4,20},{8,24},{12,28},{16,0},{20,4},{24,8},{28,12},{1,17},{... | collective-permute-start | bytes 393224 | tf_op jit(solution)/shard_map/ppermute | solution.py:302
  104.3 1.3 pad_maximum_fusion.3
  105.7 0.6 constant_dynamic-update-slice_fusion.2
  106.3 0.7 constant_dynamic-update-slice_fusion.1
  107.0 0.8 collective-permute-done.11
  107.8 0.8 constant_dynamic-update-slice_fusion
  108.6 3.4 %lows.1.lows_ref = bf16[256,1536]{1,0:T(8,128)(2,1)} custom-call(bf16[2880,256]{1,0:T(8,128)(2,1)} %bitcast.70, bf16[160,320]{1,0:T(8,128)(2,1)} %constant.167.clone.high_ref, bf16[160,320]{1,0:T(8,128)(2,1)} %constant.168.clone.low_ref), custom_call_target="tpu_custom_call" | custom-call | tf_op jit(solution)/shard_map/lows/pallas_call | solution.py:454
  111.9 1.6 %bitcast_dynamic-update-slice_fusion.1 = bf16[2880,256]{1,0:T(8,128)(2,1)} fusion(bf16[2880,256]{1,0:T(8,128)(2,1)} %bitcast_dynamic-update-slice_fusion.2, bf16[45,8,8,256]{3,2,1,0:T(8,128)(2,1)} %bitcast.71, s32[]{:T(128)S(6)} %select_n.78), kind=kLoop, calls=%fused_computation.20 | loop fusion | bytes 368644
  113.5 1.6 %bitcast_dynamic-update-slice_fusion = bf16[2880,256]{1,0:T(8,128)(2,1)} fusion(bf16[2880,256]{1,0:T(8,128)(2,1)} %bitcast_dynamic-update-slice_fusion.1, bf16[45,8,8,256]{3,2,1,0:T(8,128)(2,1)} %bitcast.72, s32[]{:T(128)S(6)} %select_n.79), kind=kLoop, calls=%fused_computation.19 | loop fusion | bytes 368644 | tf_op jit(solution)/shard_map/concatenate | solution.py:437
  115.1 1.7 %constant_dynamic-update-slice_fusion.5 = bf16[32,64,128]{2,1,0:T(8,128)(2,1)} fusion(bf16[32,64,128]{2,1,0:T(8,128)(2,1)} %get-tuple-element.47, bf16[16,64,128]{2,1,0:T(8,128)(2,1)} %collective-permute-done.12), kind=kLoop, calls=%fused_computation.40 | loop fusion | bytes 524288 | tf_op jit(solution)/shard_map/concatenate | solution.py:306
  116.8 2.8 %convert_add_fusion = f32[2880,128]{1,0:T(8,128)} fusion(f32[2880,128]{1,0:T(8,128)} %get-tuple-element.32, bf16[2880,128]{1,0:T(8,128)(2,1)} %collective-permute-done.13), kind=kLoop, calls=%fused_computation.4 | loop fusion | flops 737280 | bytes 3686400 | tf_op jit(solution)/shard_map/add | solution.py:421
  119.7 0.1 convert_add_fusion.1
  119.7 0.7 reshape.141.tiles_ref
  120.4 1.3 pad_maximum_fusion
  121.7 0.2 copy-done.6
  122.0 1.8 %fusion.8.base_ref = f32[256,512]{1,0:T(8,128)} fusion(bf16[2880,256]{1,0:T(8,128)(2,1)S(1)} %copy-done.6, bf16[2880,512]{1,0:T(8,128)(2,1)S(1)} %bitcast.78), kind=kOutput, calls=%fused_computation.57 | convolution fusion | flops 754974720 | bytes 4947968 | tf_op jit(solution)/shard_map/dot_general | solution.py:445
  123.8 8.4 %last.1 = bf16[256,512]{1,0:T(8,128)(2,1)} custom-call(s32[256]{0:T(256)} %reshape.141.tiles_ref, bf16[2048,128]{1,0:T(8,128)(2,1)} %bitcast.20.quads_ref, bf16[256,1536]{1,0:T(8,128)(2,1)} %lows.1.lows_ref, f32[256,512]{1,0:T(8,128)} %fusion.8.base_ref, bf16[256,512]{1,0:T(8,128)(2,1)} %constant.169.clone.high_ref, bf16[256,512]{1,0:T(8,128)(2,1)} %constant.170.clone.low_ref), custom_call_target="tpu_custom_call" | custom-call | tf_op jit(solution)/shard_map/last/pallas_call | solution.py:468
  (26 shorter events, 0.2 us)
Async XLA Ops:
  0.6 1.2 copy-start
  1.8 11.2 %collective-permute-start = (bf16[1,96,512]{2,1,0:T(8,128)(2,1)S(1)}, bf16[1,96,512]{2,1,0:T(8,128)(2,1)S(1)}, u32[]{:S(2)}, u32[]{:S(2)}) collective-permute-start(bf16[1,96,512]{2,1,0:T(8,128)(2,1)S(1)} %fusion.5), channel_id=1, source_target_pairs={{0,1},{1,0},{2,3},{3,2},{4,5},{5,4},{6,7},{7,6},{8,9},{9,8},{10,11... | collective-permute-start | bytes 294920 | tf_op jit(solution)/shard_map/ppermute | solution.py:302
  5.9 5.0 %copy-start.3 = (bf16[256,2880]{0,1:T(8,128)(2,1)S(1)}, bf16[256,2880]{0,1:T(8,128)(2,1)}, u32[]{:S(2)}) copy-start(bf16[256,2880]{0,1:T(8,128)(2,1)} %param.21) | copy-start | bytes 4423684
  8.9 32.2 %collective-permute-start.5 = (bf16[1280,256]{1,0:T(8,128)(2,1)}, bf16[1280,256]{1,0:T(8,128)(2,1)S(1)}, u32[]{:S(2)}, u32[]{:S(2)}) collective-permute-start(bf16[1280,256]{1,0:T(8,128)(2,1)} %pad_maximum_fusion.5), channel_id=1, source_target_pairs={{0,1},{1,0},{2,3},{3,2},{4,5},{5,4},{6,7},{7,6},{8,9},{9,8},{10,11... | collective-permute-start | bytes 1966088 | tf_op jit(solution)/shard_map/ppermute | solution.py:302
  8.9 41.8 %collective-permute-start.6 = (bf16[768,256]{1,0:T(8,128)(2,1)}, bf16[768,256]{1,0:T(8,128)(2,1)}, u32[]{:S(2)}, u32[]{:S(2)}) collective-permute-start(bf16[768,256]{1,0:T(8,128)(2,1)} %get-tuple-element.38), channel_id=1, source_target_pairs={{0,1},{1,0},{2,3},{3,2},{4,5},{5,4},{6,7},{7,6},{8,9},{9,8},{10,11... | collective-permute-start | bytes 1179656 | tf_op jit(solution)/shard_map/ppermute | solution.py:302
  13.0 22.8 %collective-permute-start.1 = (bf16[2,96,512]{2,1,0:T(8,128)(2,1)S(1)}, bf16[2,96,512]{2,1,0:T(8,128)(2,1)S(1)}, u32[]{:S(2)}, u32[]{:S(2)}) collective-permute-start(bf16[2,96,512]{2,1,0:T(8,128)(2,1)S(1)} %pad_maximum_fusion.8), channel_id=1, source_target_pairs={{0,2},{1,3},{2,0},{3,1},{4,6},{5,7},{6,4},{7,5},{8,10},{9,11},{10,... | collective-permute-start | bytes 589832 | tf_op jit(solution)/shard_map/ppermute | solution.py:302
  37.0 12.1 %collective-permute-start.2 = (bf16[1,368,512]{2,1,0:T(8,128)(2,1)S(1)}, bf16[1,368,512]{2,1,0:T(8,128)(2,1)S(1)}, u32[]{:S(2)}, u32[]{:S(2)}) collective-permute-start(bf16[1,368,512]{2,1,0:T(8,128)(2,1)S(1)} %fusion.2), channel_id=1, source_target_pairs={{0,8},{4,12},{8,0},{12,4},{16,24},{20,28},{24,16},{28,20},{1,9},{5... | collective-permute-start | bytes 1130504 | tf_op jit(solution)/shard_map/ppermute | solution.py:302
  41.1 0.8 copy-start.4
  45.7 5.5 %collective-permute-start.7 = (f32[64,128]{1,0:T(8,128)}, f32[64,128]{1,0:T(8,128)S(1)}, u32[]{:S(2)}, u32[]{:S(2)}) collective-permute-start(f32[64,128]{1,0:T(8,128)} %get-tuple-element.30), channel_id=1, source_target_pairs={{0,2},{1,3},{2,0},{3,1},{4,6},{5,7},{6,4},{7,5},{8,10},{9,11},{10,... | collective-permute-start | bytes 98312 | tf_op jit(solution)/shard_map/ppermute | solution.py:302
  49.0 55.3 %copy-start.1 = (bf16[1,368,512]{2,1,0:T(8,128)(2,1)}, bf16[1,368,512]{2,1,0:T(8,128)(2,1)S(1)}, u32[]{:S(2)}) copy-start(bf16[1,368,512]{2,1,0:T(8,128)(2,1)S(1)} %collective-permute-done.2) | copy-start | bytes 1130500
  49.1 55.2 %collective-permute-start.3 = (bf16[2,368,512]{2,1,0:T(8,128)(2,1)S(1)}, bf16[2,368,512]{2,1,0:T(8,128)(2,1)S(1)}, u32[]{:S(2)}, u32[]{:S(2)}) collective-permute-start(bf16[2,368,512]{2,1,0:T(8,128)(2,1)S(1)} %pad_maximum_fusion.4), channel_id=1, source_target_pairs={{0,16},{4,20},{8,24},{12,28},{16,0},{20,4},{24,8},{28,12},{1,17},{... | collective-permute-start | bytes 2261000 | tf_op jit(solution)/shard_map/ppermute | solution.py:302
  51.1 0.6 copy-start.5
  57.7 6.1 %collective-permute-start.8 = (bf16[1,64,128]{2,1,0:T(8,128)(2,1)}, bf16[1,64,128]{2,1,0:T(8,128)(2,1)S(1)}, u32[]{:S(2)}, u32[]{:S(2)}) collective-permute-start(bf16[1,64,128]{2,1,0:T(8,128)(2,1)} %bitcast.82), channel_id=1, source_target_pairs={{0,1},{1,0},{2,3},{3,2},{4,5},{5,4},{6,7},{7,6},{8,9},{9,8},{10,11... | collective-permute-start | bytes 49160 | tf_op jit(solution)/shard_map/ppermute | solution.py:302
  63.5 53.3 %collective-permute-start.13 = (bf16[2880,128]{1,0:T(8,128)(2,1)}, bf16[2880,128]{1,0:T(8,128)(2,1)}, u32[]{:S(2)}, u32[]{:S(2)}) collective-permute-start(bf16[2880,128]{1,0:T(8,128)(2,1)} %get-tuple-element.33), channel_id=1, source_target_pairs={{0,2},{1,3},{2,0},{3,1},{4,6},{5,7},{6,4},{7,5},{8,10},{9,11},{10,... | collective-permute-start | bytes 2211848 | tf_op jit(solution)/shard_map/ppermute | solution.py:302
  64.6 32.5 %collective-permute-start.9 = (bf16[2,64,128]{2,1,0:T(8,128)(2,1)S(1)}, bf16[2,64,128]{2,1,0:T(8,128)(2,1)S(1)}, u32[]{:S(2)}, u32[]{:S(2)}) collective-permute-start(bf16[2,64,128]{2,1,0:T(8,128)(2,1)S(1)} %pad_maximum_fusion.11), channel_id=1, source_target_pairs={{0,2},{1,3},{2,0},{3,1},{4,6},{5,7},{6,4},{7,5},{8,10},{9,11},{10,... | collective-permute-start | bytes 98312 | tf_op jit(solution)/shard_map/ppermute | solution.py:302
  97.7 4.3 %collective-permute-start.10 = (bf16[4,64,128]{2,1,0:T(8,128)(2,1)S(1)}, bf16[4,64,128]{2,1,0:T(8,128)(2,1)S(1)}, u32[]{:S(2)}, u32[]{:S(2)}) collective-permute-start(bf16[4,64,128]{2,1,0:T(8,128)(2,1)S(1)} %pad_maximum_fusion.10), channel_id=1, source_target_pairs={{0,8},{4,12},{8,0},{12,4},{16,24},{20,28},{24,16},{28,20},{1,9},{5... | collective-permute-start | bytes 196616 | tf_op jit(solution)/shard_map/ppermute | solution.py:302
  102.7 5.0 %collective-permute-start.11 = (bf16[8,64,128]{2,1,0:T(8,128)(2,1)S(1)}, bf16[8,64,128]{2,1,0:T(8,128)(2,1)S(1)}, u32[]{:S(2)}, u32[]{:S(2)}) collective-permute-start(bf16[8,64,128]{2,1,0:T(8,128)(2,1)S(1)} %pad_maximum_fusion.9), channel_id=1, source_target_pairs={{0,16},{4,20},{8,24},{12,28},{16,0},{20,4},{24,8},{28,12},{1,17},{... | collective-permute-start | bytes 393224 | tf_op jit(solution)/shard_map/ppermute | solution.py:302
  105.7 14.0 %collective-permute-start.4 = (bf16[4,368,512]{2,1,0:T(8,128)(2,1)}, bf16[4,368,512]{2,1,0:T(8,128)(2,1)S(1)}, u32[]{:S(2)}, u32[]{:S(2)}) collective-permute-start(bf16[4,368,512]{2,1,0:T(8,128)(2,1)} %pad_maximum_fusion.3), channel_id=1, source_target_pairs={{0,4},{4,0},{8,12},{12,8},{16,20},{20,16},{24,28},{28,24},{1,5},{5... | collective-permute-start | bytes 4521992 | tf_op jit(solution)/shard_map/ppermute | solution.py:302
  108.5 6.6 %collective-permute-start.12 = (bf16[16,64,128]{2,1,0:T(8,128)(2,1)}, bf16[16,64,128]{2,1,0:T(8,128)(2,1)}, u32[]{:S(2)}, u32[]{:S(2)}) collective-permute-start(bf16[16,64,128]{2,1,0:T(8,128)(2,1)} %get-tuple-element.46), channel_id=1, source_target_pairs={{0,4},{4,0},{8,12},{12,8},{16,20},{20,16},{24,28},{28,24},{1,5},{5... | collective-permute-start | bytes 786440 | tf_op jit(solution)/shard_map/ppermute | solution.py:302
  116.8 2.8 %copy-start.2 = (bf16[1,368,512]{2,1,0:T(8,128)(2,1)S(1)}, bf16[1,368,512]{2,1,0:T(8,128)(2,1)}, u32[]{:S(2)}) copy-start(bf16[1,368,512]{2,1,0:T(8,128)(2,1)} %copy-done.1) | copy-start | bytes 1130500
  120.4 1.5 %copy-start.6 = (bf16[2880,256]{1,0:T(8,128)(2,1)S(1)}, bf16[2880,256]{1,0:T(8,128)(2,1)}, u32[]{:S(2)}) copy-start(bf16[2880,256]{1,0:T(8,128)(2,1)} %bitcast_dynamic-update-slice_fusion) | copy-start | bytes 4423684
